TPU v7x, 256 devices: a whole 4x4x8 slice. The times are simulated.
256 devices in a mesh: req: 64 (over x, z, y_lo), kv: 4 (over y_hi, core).
Axes of the slice: x: 4, y: 4 (y_hi: 2, y_lo: 2; y = y_hi * 2 + y_lo), z: 8, core: 2. Of those that a mesh axis runs over, the one named last changes fastest.
Arguments:
- hidden: bfloat16 [64, 1024, 1536], P('req', 'kv'), may hold values from -6 to 6
- lengths: int32 [64], P('req'), may hold values from 1 to 2048, as said below
- key_cache: bfloat16 [64, 2048, 768], P('req', 'kv'), may hold values from -180 to 180
- value_cache: bfloat16 [64, 2048, 768], P('req', 'kv'), may hold values from -6 to 6
- norm_gain: bfloat16 [1536], replicated, may hold values from 0.099609375 to 1.8984375
- w_query: bfloat16 [1536, 1536], P('req', 'kv'), may hold values from -0.15625 to 0.15625
- w_key: bfloat16 [1536, 768], P('req', 'kv'), may hold values from -0.15625 to 0.15625
- w_value: bfloat16 [1536, 768], P('req', 'kv'), may hold values from -0.15625 to 0.15625
- w_out: bfloat16 [1536, 1536], P('req', 'kv'), may hold values from -0.15625 to 0.15625
Outputs:
- attended: bfloat16 [64, 1024, 1536], P('req', 'kv')
- new_keys: bfloat16 [64, 1024, 768], P('req', 'kv')
- new_values: bfloat16 [64, 1024, 768], P('req', 'kv')
Inputs may be any that keep to these rules, and one draw needn't show every extreme that they name: `lengths`: at least a quarter of the requests (one or more) hold more than 1792 tokens, one of them exactly 2048; the others hold fewer than 512.
All inputs are finite; a program needn't handle non-finite values.
Results may differ from a plain program's by a relative error of at most 0.011.
Values may be sent and summed in bfloat16 or wider, within the bound.
A program may use at most 192 MiB of HBM per device.

v0:
```python
import jax
import jax.numpy as jnp
from jax import lax
from jax.sharding import PartitionSpec as P

H = 16
KVH = 8
HD = 96
rope_base = 100000.0
masked_score = -1e30


def rms_norm(states, gain):
    mean_square = jnp.mean(states * states, axis=-1, keepdims=True)
    scaled = states * lax.rsqrt(mean_square + 1e-05) * gain.astype(jnp.float32)
    return scaled.astype(jnp.bfloat16)


def rotate(values, positions):
    count = values.shape[0]
    heads = values.shape[1] // HD
    half = HD // 2
    frequency = rope_base ** (-(jnp.arange(half, dtype=jnp.float32) * 2.0 / HD))
    angle = positions[:, None] * frequency[None, :]
    cosine = jnp.cos(angle)[:, None, :]
    sine = jnp.sin(angle)[:, None, :]
    shaped = values.reshape(count, heads, HD)
    first = shaped[..., :half]
    second = shaped[..., half:]
    turned = jnp.concatenate(
        [first * cosine - second * sine, second * cosine + first * sine], axis=-1
    )
    return turned.reshape(count, heads * HD)


def body(hidden, lengths, key_cache, value_cache, norm_gain, w_query, w_key, w_value, w_out):
    rows_here = hidden.shape[1]
    kv_count = lax.axis_size("kv")
    appended = rows_here * kv_count
    slots = key_cache.shape[1]
    groups = H // KVH
    scale = HD ** (-0.5)
    length = lengths[0]
    q_cols = w_query.shape[1]
    k_cols = w_key.shape[1]
    v_cols = w_value.shape[1]
    heads_here = q_cols // HD
    kv_heads_here = k_cols // HD
    normed = rms_norm(hidden[0].astype(jnp.float32), norm_gain)
    normed_all = lax.all_gather(normed, "kv", axis=0, tiled=True)
    pieces = jnp.concatenate([w_query, w_key, w_value, w_out], axis=1)
    cols = lax.all_gather(pieces, "req", axis=0, tiled=True)
    wq = cols[:, :q_cols]
    wk = cols[:, q_cols : q_cols + k_cols]
    wv = cols[:, q_cols + k_cols : q_cols + k_cols + v_cols]
    wo = cols[:, q_cols + k_cols + v_cols :]
    positions = (length + jnp.arange(appended, dtype=jnp.int32)).astype(jnp.float32)
    proj_q = jnp.dot(normed_all, wq, preferred_element_type=jnp.float32)
    proj_k = jnp.dot(normed_all, wk, preferred_element_type=jnp.float32)
    proj_v = jnp.dot(normed_all, wv, preferred_element_type=jnp.float32)
    queries = rotate(proj_q, positions).astype(jnp.bfloat16)
    keys_new = rotate(proj_k, positions).astype(jnp.bfloat16)
    values_new = proj_v.astype(jnp.bfloat16)
    new_keys = lax.all_to_all(keys_new, "kv", split_axis=0, concat_axis=1, tiled=True)
    new_values = lax.all_to_all(values_new, "kv", split_axis=0, concat_axis=1, tiled=True)
    keys_old = lax.all_to_all(key_cache[0], "kv", split_axis=1, concat_axis=0, tiled=True)
    values_old = lax.all_to_all(value_cache[0], "kv", split_axis=1, concat_axis=0, tiled=True)
    cache_slots = keys_old.shape[0]
    keys_all = jnp.concatenate([keys_old, keys_new], axis=0)
    values_all = jnp.concatenate([values_old, values_new], axis=0)
    key_count = keys_all.shape[0]
    query_index = jnp.arange(appended, dtype=jnp.int32)
    cache_live = jnp.arange(cache_slots, dtype=jnp.int32) < length
    visible = jnp.concatenate(
        [
            jnp.broadcast_to(cache_live[None, :], (appended, cache_slots)),
            query_index[None, :] <= query_index[:, None],
        ],
        axis=1,
    )
    query_heads = jnp.transpose(queries.reshape(appended, kv_heads_here, groups, HD), (1, 0, 2, 3))
    key_heads = jnp.transpose(keys_all.reshape(key_count, kv_heads_here, HD), (1, 0, 2))
    value_heads = jnp.transpose(values_all.reshape(key_count, kv_heads_here, HD), (1, 0, 2))

    def attend(operands):
        query_block, key_block, value_block = operands
        score = (
            jnp.einsum("qgd,kd->gqk", query_block, key_block, preferred_element_type=jnp.float32)
            * scale
        )
        score = jnp.where(visible[None], score, masked_score)
        peak = jnp.max(score, axis=-1)
        weights = jnp.where(visible[None], jnp.exp(score - peak[..., None]), 0.0)
        total = jnp.sum(weights, axis=-1)
        context = jnp.einsum(
            "gqk,kd->qgd",
            weights.astype(jnp.bfloat16),
            value_block,
            preferred_element_type=jnp.float32,
        )
        return context / jnp.transpose(total)[:, :, None]

    contexts = lax.map(attend, (query_heads, key_heads, value_heads))
    context = (
        jnp.transpose(contexts, (1, 0, 2, 3))
        .reshape(appended, heads_here * HD)
        .astype(jnp.bfloat16)
    )
    context_all = lax.all_gather(context, "kv", axis=1, tiled=True)
    attended_cols = jnp.dot(context_all, wo, preferred_element_type=jnp.float32).astype(
        jnp.bfloat16
    )
    attended = lax.all_to_all(attended_cols, "kv", split_axis=0, concat_axis=1, tiled=True)
    return (attended[None], new_keys[None], new_values[None])


def solution(mesh):
    return jax.shard_map(
        body,
        mesh=mesh,
        in_specs=(
            P("req", "kv", None),
            P("req"),
            P("req", "kv", None),
            P("req", "kv", None),
            P(),
            P("req", "kv"),
            P("req", "kv"),
            P("req", "kv"),
            P("req", "kv"),
        ),
        out_specs=(P("req", "kv", None), P("req", "kv", None), P("req", "kv", None)),
        check_vma=False,
    )
```

profile of v0, /device:TPU:1, one launch (start us, length us, event | category | flops | bytes accessed | tf_op | source)
XLA Modules:
  0.0 496.3 jit_solution(3980875130991210258)
XLA Ops:
  8.0 1.4 fusion.49
  9.5 2.3 fusion.51
  12.6 1.2 copy.38
  13.8 6.7 %all-to-all-start.1 = ((bf16[512,4,192]{0,2,1:T(8,128)(2,1)}), bf16[512,4,192]{0,2,1:T(8,128)(2,1)S(1)}, u32[]{:S(2)}, u32[]{:S(2)}) async-start(bf16[512,4,192]{0,2,1:T(8,128)(2,1)} %bitcast.16), calls=%async_computation.1 | async-start | bytes 1572864 | tf_op jit(solution)/shard_map/all_to_all | solution.py:66
  21.2 1.2 copy.36
  22.7 1.5 multiply_cosine_fusion
  24.2 8.6 %all-to-all-done.1 = bf16[512,4,192]{0,2,1:T(8,128)(2,1)S(1)} async-done(((bf16[512,4,192]{0,2,1:T(8,128)(2,1)}), bf16[512,4,192]{0,2,1:T(8,128)(2,1)S(1)}, u32[]{:S(2)}, u32[]{:S(2)}) %all-to-all-start.1) | async-done | bytes 786464 | tf_op jit(solution)/shard_map/all_to_all | solution.py:66
  32.8 5.2 %all-to-all-start = ((bf16[512,4,192]{0,2,1:T(8,128)(2,1)}), bf16[512,4,192]{0,2,1:T(8,128)(2,1)S(1)}, u32[]{:S(2)}, u32[]{:S(2)}) async-start(bf16[512,4,192]{0,2,1:T(8,128)(2,1)} %bitcast.9), calls=%async_computation | async-start | bytes 1572864 | tf_op jit(solution)/shard_map/all_to_all | solution.py:67
  38.0 3.5 pad_add_fusion
  42.1 1.5 concatenate.32
  43.6 14.8 %all-to-all-done = bf16[512,4,192]{0,2,1:T(8,128)(2,1)S(1)} async-done(((bf16[512,4,192]{0,2,1:T(8,128)(2,1)}), bf16[512,4,192]{0,2,1:T(8,128)(2,1)S(1)}, u32[]{:S(2)}, u32[]{:S(2)}) %all-to-all-start) | async-done | bytes 786464 | tf_op jit(solution)/shard_map/all_to_all | solution.py:67
  59.0 1.5 concatenate.27
  60.5 259.1 %all-gather.6.cloned.1.call-done = bf16[1536,1152]{1,0:T(8,128)(2,1)} async-done(((bf16[24,1152]{1,0:T(8,128)(2,1)}), bf16[1536,1152]{1,0:T(8,128)(2,1)}) %all-gather.6.cloned.1.call-update) | async-done | bytes 3538960 | tf_op jit(solution)/shard_map/all_gather | solution.py:52
  319.5 3.3 fusion.55
  323.0 2.7 fusion.53
  326.8 1.1 maximum_bitcast_fusion.1
  327.9 0.9 pad_maximum_fusion
  328.8 2.7 convolution_convert_fusion.1
  332.3 53.8 %while.10 = (s32[]{:T(128)}, bf16[2,1024,2,96]{1,3,2,0:T(8,128)(2,1)}, bf16[2,3072,96]{1,2,0:T(8,128)(2,1)S(1)}, pred[1024,3072]{0,1:T(8,128)(4,1)}, bf16[2,3072...) while((s32[]{:T(128)}, bf16[2,1024,2,96]{1,3,2,0:T(8,128)(2,1)}, ...), condition=%wide.region_4.5_spmd, body=%wide.region_1.4_spmd.sunk | while | flops 2453867520 | bytes 40126596 | solution.py:103
  332.3 19.3 %fusion.82 = (f32[2,1024]{1,0:T(2,128)S(1)}, bf16[2,1024,3072]{1,2,0:T(8,128)(2,1)}) fusion(pred[1024,3072]{0,1:T(8,128)(4,1)} %get-tuple-element.125, bf16[2,3072,96]{1,2,0:T(8,128)(2,1)} %get-tuple-element.126, s32[]{:T(128)} %get-tuple-element.115, bf16[2,1024,2,96]{1,3,2,0:T(8,128)(2,1)} %get-tuple-element.127), kind=kOutput, calls=%fused_computation.60.clone.1 | convolution fusion | flops 1245711360 | bytes 19866624 | tf_op jit(solution)/shard_map/while/body/eval_jaxpr/sub | solution.py:93
  351.6 6.7 %fusion.83 = bf16[2,1024,2,96]{1,3,2,0:T(8,128)(2,1)S(1)} fusion(bf16[2,1024,2,96]{1,3,2,0:T(8,128)(2,1)S(1)} %copy-done.9, s32[]{:T(128)} %get-tuple-element.115, bf16[2,1024,3072]{1,2,0:T(8,128)(2,1)} %get-tuple-element.106, bf16[2,3072,96]{1,2,0:T(8,128)(2,1)S(1)} %get-tuple-element.124, f32[1024,2]{0,1:T(2,128)S(1)} %bitcast.127), kind=kOutput, calls=%fused_computation.13.clone.1 | convolution fusion | flops 1208156160 | bytes 13968384 | tf_op jit(solution)/shard_map/while/body/eval_jaxpr/gqk,kd->qgd/dot_general | solution.py:95
  359.2 19.3 %fusion.82 = (f32[2,1024]{1,0:T(2,128)S(1)}, bf16[2,1024,3072]{1,2,0:T(8,128)(2,1)}) fusion(pred[1024,3072]{0,1:T(8,128)(4,1)} %get-tuple-element.125, bf16[2,3072,96]{1,2,0:T(8,128)(2,1)} %get-tuple-element.126, s32[]{:T(128)} %get-tuple-element.115, bf16[2,1024,2,96]{1,3,2,0:T(8,128)(2,1)} %get-tuple-element.127), kind=kOutput, calls=%fused_computation.60.clone.1 | convolution fusion | flops 1245711360 | bytes 19866624 | tf_op jit(solution)/shard_map/while/body/eval_jaxpr/sub | solution.py:93
  378.5 6.7 %fusion.83 = bf16[2,1024,2,96]{1,3,2,0:T(8,128)(2,1)S(1)} fusion(bf16[2,1024,2,96]{1,3,2,0:T(8,128)(2,1)S(1)} %copy-done.9, s32[]{:T(128)} %get-tuple-element.115, bf16[2,1024,3072]{1,2,0:T(8,128)(2,1)} %get-tuple-element.106, bf16[2,3072,96]{1,2,0:T(8,128)(2,1)S(1)} %get-tuple-element.124, f32[1024,2]{0,1:T(2,128)S(1)} %bitcast.127), kind=kOutput, calls=%fused_computation.13.clone.1 | convolution fusion | flops 1208156160 | bytes 13968384 | tf_op jit(solution)/shard_map/while/body/eval_jaxpr/gqk,kd->qgd/dot_general | solution.py:95
  387.2 48.5 %all-to-all-start.3 = ((bf16[4,256,192]{1,2,0:T(8,128)(2,1)}), bf16[4,256,192]{1,2,0:T(8,128)(2,1)S(1)}, u32[]{:S(2)}, u32[]{:S(2)}) async-start(bf16[4,256,192]{1,2,0:T(8,128)(2,1)} %copy.41), calls=%async_computation.3 | async-start | bytes 786432 | tf_op jit(solution)/shard_map/all_to_all | solution.py:64
  436.5 7.3 %all-to-all-done.3 = bf16[4,256,192]{1,2,0:T(8,128)(2,1)S(1)} async-done(((bf16[4,256,192]{1,2,0:T(8,128)(2,1)}), bf16[4,256,192]{1,2,0:T(8,128)(2,1)S(1)}, u32[]{:S(2)}, u32[]{:S(2)}) %all-to-all-start.3) | async-done | bytes 393248 | tf_op jit(solution)/shard_map/all_to_all | solution.py:64
  443.8 4.3 all-to-all-start.4
  448.1 18.9 %all-gather.8.cloned.1.call-done = bf16[1024,1536]{0,1:T(8,128)(2,1)} async-done(((bf16[1024,384]{0,1:T(8,128)(2,1)}), bf16[1024,1536]{0,1:T(8,128)(2,1)}) %all-gather.8.cloned.1.call-update) | async-done | bytes 3145744 | tf_op jit(solution)/shard_map/all_gather | solution.py:109
  467.0 4.9 convolution_convert_fusion
  471.9 3.7 all-to-all-start.2
  475.7 0.9 copy.43
  477.5 10.5 %all-to-all-done.2 = bf16[4,256,384]{2,1,0:T(8,128)(2,1)S(1)} async-done(((bf16[4,256,384]{2,1,0:T(8,128)(2,1)}), bf16[4,256,384]{2,1,0:T(8,128)(2,1)S(1)}, u32[]{:S(2)}, u32[]{:S(2)}) %all-to-all-start.2) | async-done | bytes 786464 | tf_op jit(solution)/shard_map/all_to_all | solution.py:113
  488.6 1.2 broadcast_in_dim.58
  (62 shorter events, 10.3 us)
Async XLA Ops:
  7.2 4.6 copy-start.11
  7.2 4.6 copy-start.13
  7.2 4.6 copy-start.14
  7.2 4.6 copy-start.12
  7.2 5.4 %copy-start.7 = (bf16[1,512,768]{2,1,0:T(8,128)(2,1)S(1)}, bf16[1,512,768]{2,1,0:T(8,128)(2,1)}, u32[]{:S(2)}) copy-start(bf16[1,512,768]{2,1,0:T(8,128)(2,1)} %param.13) | copy-start | bytes 2359300
  7.2 53.3 %all-gather.4.cloned.1.call-start = ((), (), s32[]{:S(2)}) async-start(), calls=%async_computation.5 | async-start | bytes 3932160 | tf_op jit(solution)/shard_map/all_gather | solution.py:50
  8.0 13.1 %copy-start.8 = (bf16[1,512,768]{2,1,0:T(8,128)(2,1)S(1)}, bf16[1,512,768]{2,1,0:T(8,128)(2,1)}, u32[]{:S(2)}) copy-start(bf16[1,512,768]{2,1,0:T(8,128)(2,1)} %param.14) | copy-start | bytes 2359300
  11.8 307.8 %all-gather.6.cloned.1.call-start = ((), (), s32[]{:S(2)}) async-start(), calls=%async_computation.6 | async-start | bytes 3594240 | tf_op jit(solution)/shard_map/all_gather | solution.py:52
  13.8 19.0 %all-to-all-start.1 = ((bf16[512,4,192]{0,2,1:T(8,128)(2,1)}), bf16[512,4,192]{0,2,1:T(8,128)(2,1)S(1)}, u32[]{:S(2)}, u32[]{:S(2)}) async-start(bf16[512,4,192]{0,2,1:T(8,128)(2,1)} %bitcast.16), calls=%async_computation.1 | async-start | bytes 1572864 | tf_op jit(solution)/shard_map/all_to_all | solution.py:66
  32.8 25.6 %all-to-all-start = ((bf16[512,4,192]{0,2,1:T(8,128)(2,1)}), bf16[512,4,192]{0,2,1:T(8,128)(2,1)S(1)}, u32[]{:S(2)}, u32[]{:S(2)}) async-start(bf16[512,4,192]{0,2,1:T(8,128)(2,1)} %bitcast.9), calls=%async_computation | async-start | bytes 1572864 | tf_op jit(solution)/shard_map/all_to_all | solution.py:67
  38.0 429.0 %all-gather.8.cloned.1.call-start = ((), (), s32[]{:S(2)}) async-start(), calls=%async_computation.7 | async-start | bytes 3932160 | tf_op jit(solution)/shard_map/all_gather | solution.py:109
  60.5 262.3 %copy-start.3 = (f32[1024,48]{0,1:T(8,128)S(1)}, f32[1024,48]{0,1:T(8,128)}, u32[]{:S(2)}) copy-start(f32[1024,48]{0,1:T(8,128)} %get-tuple-element.63) | copy-start | bytes 589828
  60.5 262.3 %copy-start.4 = (f32[1024,48]{0,1:T(8,128)S(1)}, f32[1024,48]{0,1:T(8,128)}, u32[]{:S(2)}) copy-start(f32[1024,48]{0,1:T(8,128)} %get-tuple-element.64) | copy-start | bytes 589828
  60.5 262.5 %copy-start = (bf16[1024,1536]{1,0:T(8,128)(2,1)S(1)}, bf16[1024,1536]{1,0:T(8,128)(2,1)}, u32[]{:S(2)}) copy-start(bf16[1024,1536]{1,0:T(8,128)(2,1)} %all-gather.4.cloned.1.call-done) | copy-start | bytes 9437188
  325.7 1.1 copy-start.1
  327.9 3.6 copy-start.2
  331.5 0.8 copy-start.5
  332.3 19.3 %copy-start.9 = (bf16[2,1024,2,96]{1,3,2,0:T(8,128)(2,1)S(1)}, bf16[2,1024,2,96]{1,3,2,0:T(8,128)(2,1)}, u32[]{:S(2)}) copy-start(bf16[2,1024,2,96]{1,3,2,0:T(8,128)(2,1)} %get-tuple-element.116) | copy-start | bytes 2359300 | tf_op jit(solution)/shard_map/while
  358.3 0.9 copy-start.10
  359.2 19.3 %copy-start.9 = (bf16[2,1024,2,96]{1,3,2,0:T(8,128)(2,1)S(1)}, bf16[2,1024,2,96]{1,3,2,0:T(8,128)(2,1)}, u32[]{:S(2)}) copy-start(bf16[2,1024,2,96]{1,3,2,0:T(8,128)(2,1)} %get-tuple-element.116) | copy-start | bytes 2359300 | tf_op jit(solution)/shard_map/while
  385.2 0.9 copy-start.10
  386.1 49.6 %copy-start.6 = (bf16[1024,192]{0,1:T(8,128)(2,1)S(1)}, bf16[1024,192]{0,1:T(8,128)(2,1)}, u32[]{:S(2)}) copy-start(bf16[1024,192]{0,1:T(8,128)(2,1)} %copy-done.5) | copy-start | bytes 1179652
  387.2 56.6 %all-to-all-start.3 = ((bf16[4,256,192]{1,2,0:T(8,128)(2,1)}), bf16[4,256,192]{1,2,0:T(8,128)(2,1)S(1)}, u32[]{:S(2)}, u32[]{:S(2)}) async-start(bf16[4,256,192]{1,2,0:T(8,128)(2,1)} %copy.41), calls=%async_computation.3 | async-start | bytes 786432 | tf_op jit(solution)/shard_map/all_to_all | solution.py:64
  443.8 28.2 %all-to-all-start.4 = ((bf16[4,256,192]{1,2,0:T(8,128)(2,1)}), bf16[4,256,192]{1,2,0:T(8,128)(2,1)S(1)}, u32[]{:S(2)}, u32[]{:S(2)}) async-start(bf16[4,256,192]{1,2,0:T(8,128)(2,1)} %bitcast.97), calls=%async_computation.4 | async-start | bytes 786432 | tf_op jit(solution)/shard_map/all_to_all | solution.py:65
  471.9 16.0 %all-to-all-start.2 = ((bf16[4,256,384]{2,1,0:T(8,128)(2,1)}), bf16[4,256,384]{2,1,0:T(8,128)(2,1)S(1)}, u32[]{:S(2)}, u32[]{:S(2)}) async-start(bf16[4,256,384]{2,1,0:T(8,128)(2,1)} %bitcast.25), calls=%async_computation.2 | async-start | bytes 1572864 | tf_op jit(solution)/shard_map/all_to_all | solution.py:113
Sparse Core Ops, SparseCore 0:
  11.9 47.5 all-gather.3
  61.2 258.2 all-gather.5
  386.2 80.7 all-gather.7
where the time goes:
time: 497 us; the launch traced here: 496 us
  waiting for transfers between devices  319 us (64%)
  starting transfers between devices  68.6 us (14%)
  matrix products  65.6 us (13%)
  local copies, waits for them, and re-layouts  16 us (3%)
  between operations  14.6 us (3%)
  other arithmetic  12.3 us (2%)
    all_gather x1, waiting for transfers between devices, body(): cols = lax.all_gather(pieces, 'req', axis=0, tiled=True)  259 us
    all_to_all x1, starting transfers between devices, body(): lax.all_to_all(keys_new, 'kv', split_axis=0, concat_axis=1, tiled=True)  48.5 us
    sub x2, matrix products, attend(): weights = jnp.where(visible[None], jnp.exp(score - peak[..., None]), 0.0)  38.6 us
    all_gather x1, waiting for transfers between devices, body(): context_all = lax.all_gather(context, 'kv', axis=1, tiled=True)  18.9 us
    all_to_all x1, waiting for transfers between devices, body(): lax.all_to_all(value_cache[0], 'kv', split_axis=1, concat_axis=0, tiled=T...  14.8 us
    dot_general x2, matrix products, attend(): jnp.einsum('gqk,kd->qgd', weights.astype(jnp.bfloat16), value_block, pref...  13.4 us
    all_to_all x1, waiting for transfers between devices, body(): lax.all_to_all(attended_cols, 'kv', split_axis=0, concat_axis=1, tiled=True)  10.5 us
  transfers between devices with their start and end apart: 8, of which 6 were waited for; matrix products, arithmetic and copies ran while one was open for 4% of the time, Pallas kernels for 0%

commit v1 on v0

--- a/solution.py
+++ b/solution.py
@@ -49,7 +49,8 @@
     normed = rms_norm(hidden[0].astype(jnp.float32), norm_gain)
     normed_all = lax.all_gather(normed, "kv", axis=0, tiled=True)
     pieces = jnp.concatenate([w_query, w_key, w_value, w_out], axis=1)
-    cols = lax.all_gather(pieces, "req", axis=0, tiled=True)
+    sent = jnp.stack([pieces] * lax.axis_size("req"))
+    cols = jnp.concatenate(lax.all_to_all(sent, "req", 0, 0), axis=0)
     wq = cols[:, :q_cols]
     wk = cols[:, q_cols : q_cols + k_cols]
     wv = cols[:, q_cols + k_cols : q_cols + k_cols + v_cols]

time: 497 us -> 273 us (0.55)
  waiting for transfers between devices: 319 us -> 112 us
  starting transfers between devices: 68.6 us -> 39.1 us
  local copies, waits for them, and re-layouts: 16 us -> 27.7 us
    all_gather x1 -> x0, waiting for transfers between devices: 259 us -> none  [body(): cols = lax.all_gather(pieces, 'req', axis=0, tiled=True)]
    all_to_all x1, starting transfers between devices: 48.5 us -> 7.84 us  [body(): lax.all_to_all(keys_new, 'kv', split_axis=0, concat_axis=1, tiled=True)]
    all_gather x1, waiting for transfers between devices: 0.01 us -> 33.5 us  [body(): normed_all = lax.all_gather(normed, 'kv', axis=0, tiled=True)]
    all_to_all x0 -> x1, waiting for transfers between devices: none -> 26.2 us  [body(): cols = jnp.concatenate(lax.all_to_all(sent, 'req', 0, 0), axis=0)]
    all_to_all x0 -> x1, starting transfers between devices: none -> 11.2 us  [body(): cols = jnp.concatenate(lax.all_to_all(sent, 'req', 0, 0), axis=0)]
    all_gather x1, waiting for transfers between devices: 18.9 us -> 9.6 us  [body(): context_all = lax.all_gather(context, 'kv', axis=1, tiled=True)]
  transfers between devices with their start and end apart: 8 -> 8, of which waited for: 6 -> 7; matrix products, arithmetic and copies ran while one was open for 4% -> 13% of each run, Pallas kernels for 0% -> 0%
where the time goes in v1:
time: 273 us; the launch traced here: 271 us
  waiting for transfers between devices  112 us (41%)
  matrix products  64.5 us (24%)
  starting transfers between devices  39.1 us (14%)
  local copies, waits for them, and re-layouts  27.7 us (10%)
  between operations  14.9 us (5%)
  other arithmetic  12.6 us (5%)
    sub x2, matrix products, attend(): weights = jnp.where(visible[None], jnp.exp(score - peak[..., None]), 0.0)  38.5 us
    all_gather x1, waiting for transfers between devices, body(): normed_all = lax.all_gather(normed, 'kv', axis=0, tiled=True)  33.5 us
    all_to_all x1, waiting for transfers between devices, body(): cols = jnp.concatenate(lax.all_to_all(sent, 'req', 0, 0), axis=0)  26.2 us
    dot_general x2, matrix products, attend(): jnp.einsum('gqk,kd->qgd', weights.astype(jnp.bfloat16), value_block, pref...  15.3 us
    all_to_all x1, waiting for transfers between devices, body(): lax.all_to_all(value_cache[0], 'kv', split_axis=1, concat_axis=0, tiled=T...  12.2 us
    all_to_all x1, starting transfers between devices, body(): cols = jnp.concatenate(lax.all_to_all(sent, 'req', 0, 0), axis=0)  11.2 us
    all_to_all x1, waiting for transfers between devices, body(): lax.all_to_all(key_cache[0], 'kv', split_axis=1, concat_axis=0, tiled=True)  11.1 us
    all_to_all x1, waiting for transfers between devices, body(): lax.all_to_all(keys_new, 'kv', split_axis=0, concat_axis=1, tiled=True)  10.8 us
  transfers between devices with their start and end apart: 8, of which 7 were waited for; matrix products, arithmetic and copies ran while one was open for 13% of the time, Pallas kernels for 0%

profile of v1, /device:TPU:1, one launch (start us, length us, event | category | flops | bytes accessed | tf_op | source)
XLA Modules:
  0.0 270.8 jit_solution(11472854711332432233)
XLA Ops:
  7.2 2.4 copy.38
  9.6 6.7 %all-to-all-start.2 = ((bf16[512,4,192]{0,2,1:T(8,128)(2,1)}), bf16[512,4,192]{0,2,1:T(8,128)(2,1)S(1)}, u32[]{:S(2)}, u32[]{:S(2)}) async-start(bf16[512,4,192]{0,2,1:T(8,128)(2,1)} %bitcast.17), calls=%async_computation.2 | async-start | bytes 1572864 | tf_op jit(solution)/shard_map/all_to_all | solution.py:67
  17.5 11.1 %all-to-all-done.2 = bf16[512,4,192]{0,2,1:T(8,128)(2,1)S(1)} async-done(((bf16[512,4,192]{0,2,1:T(8,128)(2,1)}), bf16[512,4,192]{0,2,1:T(8,128)(2,1)S(1)}, u32[]{:S(2)}, u32[]{:S(2)}) %all-to-all-start.2) | async-done | bytes 786464 | tf_op jit(solution)/shard_map/all_to_all | solution.py:67
  28.6 4.3 %all-to-all-start = ((bf16[512,4,192]{0,2,1:T(8,128)(2,1)}), bf16[512,4,192]{0,2,1:T(8,128)(2,1)S(1)}, u32[]{:S(2)}, u32[]{:S(2)}) async-start(bf16[512,4,192]{0,2,1:T(8,128)(2,1)} %bitcast.9), calls=%async_computation | async-start | bytes 1572864 | tf_op jit(solution)/shard_map/all_to_all | solution.py:68
  33.0 12.2 %all-to-all-done = bf16[512,4,192]{0,2,1:T(8,128)(2,1)S(1)} async-done(((bf16[512,4,192]{0,2,1:T(8,128)(2,1)}), bf16[512,4,192]{0,2,1:T(8,128)(2,1)S(1)}, u32[]{:S(2)}, u32[]{:S(2)}) %all-to-all-start) | async-done | bytes 786464 | tf_op jit(solution)/shard_map/all_to_all | solution.py:68
  45.2 2.0 stack.2
  47.2 11.2 %all-to-all-start.1 = ((bf16[64,24,1152]{2,1,0:T(8,128)(2,1)}), bf16[64,24,1152]{2,1,0:T(8,128)(2,1)S(1)}, u32[]{:S(2)}, u32[]{:S(2)}) async-start(bf16[64,24,1152]{2,1,0:T(8,128)(2,1)} %stack.2), calls=%async_computation.1 | async-start | bytes 7077888 | tf_op jit(solution)/shard_map/all_to_all | solution.py:53
  59.9 2.3 fusion.51
  64.9 3.5 %pad_add_fusion = pred[1024,3072]{0,1:T(8,128)(4,1)} fusion(pred[1024,1024]{0,1:T(8,128)(4,1)S(1)} %iota_compare_fusion, pred[3072]{0:T(1024)(128)(4,1)S(1)} %pad.6.clone), kind=kLoop, calls=%fused_computation.30 | loop fusion | flops 3145728 | bytes 4197376 | tf_op jit(solution)/shard_map/concatenate | solution.py:75
  70.0 2.8 %concatenate.32 = bf16[2048,2,96]{0,2,1:T(8,128)(2,1)} reshape(bf16[4,512,192]{1,0,2:T(4,128)(2,1)} %copy.39) | data formatting | bytes 1572864 | tf_op jit(solution)/shard_map/concatenate | solution.py:70
  72.8 2.8 %copy.37 = bf16[4,512,192]{1,0,2:T(4,128)(2,1)} copy(bf16[4,512,192]{1,2,0:T(8,128)(2,1)} %bitcast.123) | data formatting | bytes 1572864 | tf_op jit(solution)/shard_map/all_to_all | solution.py:68
  75.6 2.9 %concatenate.27 = bf16[2048,2,96]{0,2,1:T(8,128)(2,1)} reshape(bf16[4,512,192]{1,0,2:T(4,128)(2,1)} %copy.37) | data formatting | bytes 1572864 | tf_op jit(solution)/shard_map/concatenate | solution.py:71
  78.4 33.5 %all-gather.3.cloned.1.call-done = bf16[1024,1536]{1,0:T(8,128)(2,1)} async-done(((bf16[256,1536]{1,0:T(8,128)(2,1)}), bf16[1024,1536]{1,0:T(8,128)(2,1)}) %all-gather.3.cloned.1.call-update) | async-done | bytes 3145744 | tf_op jit(solution)/shard_map/all_gather | solution.py:50
  112.0 26.2 %all-to-all-done.1 = bf16[64,24,1152]{2,1,0:T(8,128)(2,1)S(1)} async-done(((bf16[64,24,1152]{2,1,0:T(8,128)(2,1)}), bf16[64,24,1152]{2,1,0:T(8,128)(2,1)S(1)}, u32[]{:S(2)}, u32[]{:S(2)}) %all-to-all-start.1) | async-done | bytes 3538976 | tf_op jit(solution)/shard_map/all_to_all | solution.py:53
  138.2 3.2 %fusion.55 = f32[1024,192]{0,1:T(8,128)S(1)} fusion(bf16[1024,1536]{1,0:T(8,128)(2,1)} %all-gather.3.cloned.1.call-done, bf16[1536,1152]{1,0:T(8,128)(2,1)S(1)} %bitcast.117), kind=kOutput, calls=%fused_computation.44 | convolution fusion | flops 603979776 | bytes 4718592 | tf_op jit(solution)/shard_map/dot_general | solution.py:60
  148.9 53.8 %while.10 = (s32[]{:T(128)}, bf16[2,1024,2,96]{1,3,2,0:T(8,128)(2,1)}, bf16[2,3072,96]{1,2,0:T(8,128)(2,1)}, pred[1024,3072]{0,1:T(8,128)(4,1)}, bf16[2,3072,96]...) while((s32[]{:T(128)}, bf16[2,1024,2,96]{1,3,2,0:T(8,128)(2,1)}, ...), condition=%wide.region_4.5_spmd, body=%wide.region_1.4_spmd.sunk | while | flops 2453867520 | bytes 33835084 | solution.py:104
  148.9 19.2 %fusion.82 = (f32[2,1024]{1,0:T(2,128)S(1)}, bf16[2,1024,3072]{1,2,0:T(8,128)(2,1)}) fusion(pred[1024,3072]{0,1:T(8,128)(4,1)} %get-tuple-element.125, bf16[2,3072,96]{1,2,0:T(8,128)(2,1)} %get-tuple-element.126, s32[]{:T(128)} %get-tuple-element.115, bf16[2,1024,2,96]{1,3,2,0:T(8,128)(2,1)} %get-tuple-element.127), kind=kOutput, calls=%fused_computation.60.clone.1 | convolution fusion | flops 1245711360 | bytes 19866624 | tf_op jit(solution)/shard_map/while/body/eval_jaxpr/sub | solution.py:94
  168.1 7.6 %fusion.83 = bf16[2,1024,2,96]{1,3,2,0:T(8,128)(2,1)} fusion(bf16[2,1024,2,96]{1,3,2,0:T(8,128)(2,1)} %get-tuple-element.116, s32[]{:T(128)} %get-tuple-element.115, bf16[2,1024,3072]{1,2,0:T(8,128)(2,1)} %get-tuple-element.106, bf16[2,3072,96]{1,2,0:T(8,128)(2,1)} %get-tuple-element.124, f32[1024,2]{0,1:T(2,128)S(1)} %bitcast.132), kind=kOutput, calls=%fused_computation.13.clone.1 | convolution fusion | flops 1208156160 | bytes 13968384 | tf_op jit(solution)/shard_map/while/body/eval_jaxpr/gqk,kd->qgd/dot_general | solution.py:96
  175.7 19.3 %fusion.82 = (f32[2,1024]{1,0:T(2,128)S(1)}, bf16[2,1024,3072]{1,2,0:T(8,128)(2,1)}) fusion(pred[1024,3072]{0,1:T(8,128)(4,1)} %get-tuple-element.125, bf16[2,3072,96]{1,2,0:T(8,128)(2,1)} %get-tuple-element.126, s32[]{:T(128)} %get-tuple-element.115, bf16[2,1024,2,96]{1,3,2,0:T(8,128)(2,1)} %get-tuple-element.127), kind=kOutput, calls=%fused_computation.60.clone.1 | convolution fusion | flops 1245711360 | bytes 19866624 | tf_op jit(solution)/shard_map/while/body/eval_jaxpr/sub | solution.py:94
  195.0 7.6 %fusion.83 = bf16[2,1024,2,96]{1,3,2,0:T(8,128)(2,1)} fusion(bf16[2,1024,2,96]{1,3,2,0:T(8,128)(2,1)} %get-tuple-element.116, s32[]{:T(128)} %get-tuple-element.115, bf16[2,1024,3072]{1,2,0:T(8,128)(2,1)} %get-tuple-element.106, bf16[2,3072,96]{1,2,0:T(8,128)(2,1)} %get-tuple-element.124, f32[1024,2]{0,1:T(2,128)S(1)} %bitcast.132), kind=kOutput, calls=%fused_computation.13.clone.1 | convolution fusion | flops 1208156160 | bytes 13968384 | tf_op jit(solution)/shard_map/while/body/eval_jaxpr/gqk,kd->qgd/dot_general | solution.py:96
  202.7 2.0 convert_element_type.62
  204.7 1.8 copy.41
  206.5 7.8 %all-to-all-start.4 = ((bf16[4,256,192]{1,2,0:T(8,128)(2,1)}), bf16[4,256,192]{1,2,0:T(8,128)(2,1)}, u32[]{:S(2)}, u32[]{:S(2)}) async-start(bf16[4,256,192]{1,2,0:T(8,128)(2,1)} %copy.41), calls=%async_computation.4 | async-start | bytes 786432 | tf_op jit(solution)/shard_map/all_to_all | solution.py:65
  214.3 1.8 copy.48
  216.1 10.8 %all-to-all-done.4 = bf16[4,256,192]{1,2,0:T(8,128)(2,1)} async-done(((bf16[4,256,192]{1,2,0:T(8,128)(2,1)}), bf16[4,256,192]{1,2,0:T(8,128)(2,1)}, u32[]{:S(2)}, u32[]{:S(2)}) %all-to-all-start.4) | async-done | bytes 393248 | tf_op jit(solution)/shard_map/all_to_all | solution.py:65
  226.9 5.1 %all-to-all-start.5 = ((bf16[4,256,192]{1,2,0:T(8,128)(2,1)}), bf16[4,256,192]{1,2,0:T(8,128)(2,1)}, u32[]{:S(2)}, u32[]{:S(2)}) async-start(bf16[4,256,192]{1,2,0:T(8,128)(2,1)} %bitcast.127), calls=%async_computation.5 | async-start | bytes 786432 | tf_op jit(solution)/shard_map/all_to_all | solution.py:66
  232.0 9.6 %all-gather.5.cloned.1.call-done = bf16[1024,1536]{0,1:T(8,128)(2,1)} async-done(((bf16[1024,384]{0,1:T(8,128)(2,1)}), bf16[1024,1536]{0,1:T(8,128)(2,1)}) %all-gather.5.cloned.1.call-update) | async-done | bytes 3145744 | tf_op jit(solution)/shard_map/all_gather | solution.py:110
  241.6 4.6 %convolution_convert_fusion = bf16[1024,384]{1,0:T(8,128)(2,1)} fusion(bf16[1024,1536]{0,1:T(8,128)(2,1)} %all-gather.5.cloned.1.call-done, bf16[1536,1152]{1,0:T(8,128)(2,1)S(1)} %bitcast.120), kind=kOutput, calls=%fused_computation.37 | convolution fusion | flops 1208352768 | bytes 5111808 | tf_op jit(solution)/shard_map/dot_general | solution.py:111
  246.2 3.7 %all-to-all-start.3 = ((bf16[4,256,384]{2,1,0:T(8,128)(2,1)}), bf16[4,256,384]{2,1,0:T(8,128)(2,1)S(1)}, u32[]{:S(2)}, u32[]{:S(2)}) async-start(bf16[4,256,384]{2,1,0:T(8,128)(2,1)} %bitcast.131), calls=%async_computation.3 | async-start | bytes 1572864 | tf_op jit(solution)/shard_map/all_to_all | solution.py:114
  249.9 1.9 copy.43
  251.8 1.9 copy.44
  253.7 8.5 %all-to-all-done.3 = bf16[4,256,384]{2,1,0:T(8,128)(2,1)S(1)} async-done(((bf16[4,256,384]{2,1,0:T(8,128)(2,1)}), bf16[4,256,384]{2,1,0:T(8,128)(2,1)S(1)}, u32[]{:S(2)}, u32[]{:S(2)}) %all-to-all-start.3) | async-done | bytes 786464 | tf_op jit(solution)/shard_map/all_to_all | solution.py:114
  (60 shorter events, 15.5 us)
Async XLA Ops:
  7.2 9.1 %copy-start.10 = (bf16[1,512,768]{2,1,0:T(8,128)(2,1)S(1)}, bf16[1,512,768]{2,1,0:T(8,128)(2,1)}, u32[]{:S(2)}) copy-start(bf16[1,512,768]{2,1,0:T(8,128)(2,1)} %param.14) | copy-start | bytes 2359300
  7.2 25.8 %copy-start.11 = (bf16[24,384]{1,0:T(8,128)(2,1)S(1)}, bf16[24,384]{1,0:T(8,128)(2,1)}, u32[]{:S(2)}) copy-start(bf16[24,384]{1,0:T(8,128)(2,1)} %param.16) | copy-start | bytes 55300
  7.2 25.7 %copy-start.13 = (bf16[24,192]{1,0:T(8,128)(2,1)S(1)}, bf16[24,192]{1,0:T(8,128)(2,1)}, u32[]{:S(2)}) copy-start(bf16[24,192]{1,0:T(8,128)(2,1)} %param.17) | copy-start | bytes 27652
  7.2 25.7 %copy-start.14 = (bf16[24,192]{1,0:T(8,128)(2,1)S(1)}, bf16[24,192]{1,0:T(8,128)(2,1)}, u32[]{:S(2)}) copy-start(bf16[24,192]{1,0:T(8,128)(2,1)} %param.18) | copy-start | bytes 27652
  7.2 25.7 %copy-start.12 = (bf16[24,384]{1,0:T(8,128)(2,1)S(1)}, bf16[24,384]{1,0:T(8,128)(2,1)}, u32[]{:S(2)}) copy-start(bf16[24,384]{1,0:T(8,128)(2,1)} %param.19) | copy-start | bytes 55300
  9.6 19.0 %all-to-all-start.2 = ((bf16[512,4,192]{0,2,1:T(8,128)(2,1)}), bf16[512,4,192]{0,2,1:T(8,128)(2,1)S(1)}, u32[]{:S(2)}, u32[]{:S(2)}) async-start(bf16[512,4,192]{0,2,1:T(8,128)(2,1)} %bitcast.17), calls=%async_computation.2 | async-start | bytes 1572864 | tf_op jit(solution)/shard_map/all_to_all | solution.py:67
  28.6 18.6 %copy-start.2 = (bf16[512,4,192]{0,2,1:T(8,128)(2,1)}, bf16[512,4,192]{0,2,1:T(8,128)(2,1)S(1)}, u32[]{:S(2)}) copy-start(bf16[512,4,192]{0,2,1:T(8,128)(2,1)S(1)} %all-to-all-done.2) | copy-start | bytes 2359300
  28.6 16.6 %all-to-all-start = ((bf16[512,4,192]{0,2,1:T(8,128)(2,1)}), bf16[512,4,192]{0,2,1:T(8,128)(2,1)S(1)}, u32[]{:S(2)}, u32[]{:S(2)}) async-start(bf16[512,4,192]{0,2,1:T(8,128)(2,1)} %bitcast.9), calls=%async_computation | async-start | bytes 1572864 | tf_op jit(solution)/shard_map/all_to_all | solution.py:68
  45.2 2.0 copy-start.4
  47.2 11.2 %copy-start.15 = (bf16[1536]{0:T(1024)(128)(2,1)S(1)}, bf16[1536]{0:T(1024)(128)(2,1)}, u32[]{:S(2)}) copy-start(bf16[1536]{0:T(1024)(128)(2,1)} %param.15) | copy-start | bytes 9220
  47.2 91.0 %all-to-all-start.1 = ((bf16[64,24,1152]{2,1,0:T(8,128)(2,1)}), bf16[64,24,1152]{2,1,0:T(8,128)(2,1)S(1)}, u32[]{:S(2)}, u32[]{:S(2)}) async-start(bf16[64,24,1152]{2,1,0:T(8,128)(2,1)} %stack.2), calls=%async_computation.1 | async-start | bytes 7077888 | tf_op jit(solution)/shard_map/all_to_all | solution.py:53
  58.4 53.6 %all-gather.3.cloned.1.call-start = ((), (), s32[]{:S(2)}) async-start(), calls=%async_computation.6 | async-start | bytes 3932160 | tf_op jit(solution)/shard_map/all_gather | solution.py:50
  62.1 179.4 %all-gather.5.cloned.1.call-start = ((), (), s32[]{:S(2)}) async-start(), calls=%async_computation.7 | async-start | bytes 3932160 | tf_op jit(solution)/shard_map/all_gather | solution.py:110
  63.0 5.4 %copy-start.3 = (bf16[512,4,192]{0,2,1:T(8,128)(2,1)S(1)}, bf16[512,4,192]{0,2,1:T(8,128)(2,1)}, u32[]{:S(2)}) copy-start(bf16[512,4,192]{0,2,1:T(8,128)(2,1)} %copy-done.2) | copy-start | bytes 2359300
  138.2 3.2 %copy-start.7 = (f32[1024,48]{0,1:T(8,128)S(1)}, f32[1024,48]{0,1:T(8,128)}, u32[]{:S(2)}) copy-start(f32[1024,48]{0,1:T(8,128)} %get-tuple-element.63) | copy-start | bytes 589828
  138.2 3.2 %copy-start.8 = (f32[1024,48]{0,1:T(8,128)S(1)}, f32[1024,48]{0,1:T(8,128)}, u32[]{:S(2)}) copy-start(f32[1024,48]{0,1:T(8,128)} %get-tuple-element.64) | copy-start | bytes 589828
  138.2 3.4 %copy-start.1 = (bf16[1024,1536]{1,0:T(8,128)(2,1)S(1)}, bf16[1024,1536]{1,0:T(8,128)(2,1)}, u32[]{:S(2)}) copy-start(bf16[1024,1536]{1,0:T(8,128)(2,1)} %all-gather.3.cloned.1.call-done) | copy-start | bytes 9437188
  143.1 1.1 copy-start.6
  143.4 0.7 copy-start
  145.3 2.4 copy-start.5
  147.7 1.2 copy-start.9
  206.5 20.4 %all-to-all-start.4 = ((bf16[4,256,192]{1,2,0:T(8,128)(2,1)}), bf16[4,256,192]{1,2,0:T(8,128)(2,1)}, u32[]{:S(2)}, u32[]{:S(2)}) async-start(bf16[4,256,192]{1,2,0:T(8,128)(2,1)} %copy.41), calls=%async_computation.4 | async-start | bytes 786432 | tf_op jit(solution)/shard_map/all_to_all | solution.py:65
  226.9 19.3 %all-to-all-start.5 = ((bf16[4,256,192]{1,2,0:T(8,128)(2,1)}), bf16[4,256,192]{1,2,0:T(8,128)(2,1)}, u32[]{:S(2)}, u32[]{:S(2)}) async-start(bf16[4,256,192]{1,2,0:T(8,128)(2,1)} %bitcast.127), calls=%async_computation.5 | async-start | bytes 786432 | tf_op jit(solution)/shard_map/all_to_all | solution.py:66
  246.2 16.0 %all-to-all-start.3 = ((bf16[4,256,384]{2,1,0:T(8,128)(2,1)}), bf16[4,256,384]{2,1,0:T(8,128)(2,1)S(1)}, u32[]{:S(2)}, u32[]{:S(2)}) async-start(bf16[4,256,384]{2,1,0:T(8,128)(2,1)} %bitcast.131), calls=%async_computation.3 | async-start | bytes 1572864 | tf_op jit(solution)/shard_map/all_to_all | solution.py:114
Sparse Core Ops, SparseCore 0:
  62.3 49.6 all-gather.2
  202.8 38.7 all-gather.4
